TPU v7x, 512 devices: a whole 4x4x16 slice. The times are simulated.
512 devices in a mesh: lat: 32 (over z, core), lev: 16 (over x, y).
Axes of the slice: x: 4, y: 4, z: 16, core: 2. Of those that a mesh axis runs over, the one named last changes fastest.
Arguments:
- zonal_wind: float32 [64, 256, 2880], P('lev', 'lat'), may hold values from -1 to 1
- merid_wind: float32 [64, 256, 2880], P('lev', 'lat'), may hold values from -1 to 1
- thickness: float32 [64, 256, 2880], P('lev', 'lat'), may hold values from 0.6 to 1.8
- potential_temp: float32 [64, 256, 2880], P('lev', 'lat'), may hold values from 0.5 to 2
- cutoff: int32 [32], replicated, may hold values from 4 to 255, as said below
- sigma_weights: float32 [64], replicated, may hold values from 0.5 to 2
Outputs:
- remapped_wind: float32 [64, 256, 2880], P(None, 'lat', 'lev')
- remapped_temp: float32 [64, 256, 2880], P(None, 'lat', 'lev')
Inputs may be any that keep to these rules, and one draw needn't show every extreme that they name: `cutoff`: cutoff wavenumber of each filtered row, southern rows in row order, then northern rows in row order.
All inputs are finite; a program needn't handle non-finite values.
Results may differ from a plain program's by a relative error of at most 0.0003.
Values sent between devices are 32-bit elements; how exact they have to be, the bound alone decides.
No kernel may reach another device: no remote copies, remote signals or barrier semaphores. Data moves between devices by JAX's collectives and lax.ppermute only.
A program may use at most 64 MiB of HBM per device.

v0:
```python
import math
import jax
import jax.numpy as jnp
from jax import lax
from jax.sharding import PartitionSpec as P

POLAR_BANDS = 2
KMAX = 256
COURANT = 0.02
PRESSURE_COEF = 0.05
HIGHEST = lax.Precision.HIGHEST


def with_halo(x, sides, width):
    for axis, dim in sides:
        count, length = (lax.axis_size(axis), x.shape[dim])
        up = [(i, (i + 1) % count) for i in range(count - 1)]
        down = [(j, i) for i, j in up]
        last = lax.slice_in_dim(x, length - width, length, axis=dim)
        first = lax.slice_in_dim(x, 0, width, axis=dim)
        before = lax.ppermute(last, axis, up)
        after = lax.ppermute(first, axis, down)
        x = jnp.concatenate([before, x, after], axis=dim)
    return x


def prefix(part, axis, combine, identity):
    place = lax.axis_index(axis)
    gathered = lax.all_gather(part, axis)
    state = jnp.zeros_like(part) + jnp.asarray(identity, part.dtype)

    def one(lap, state):
        return combine(state, lax.dynamic_index_in_dim(gathered, lap, 0, False))

    return lax.fori_loop(0, place, one, state)


def flux_zonal(quantity, wind):
    face_wind = 0.5 * (wind + jnp.roll(wind, 1, axis=-1))
    face_flux = face_wind * 0.5 * (quantity + jnp.roll(quantity, 1, axis=-1))
    return jnp.roll(face_flux, -1, axis=-1) - face_flux


def flux_merid(padded_field, padded_wind):
    face_flux = (
        0.25
        * (padded_wind[:, :-1] + padded_wind[:, 1:])
        * (padded_field[:, :-1] + padded_field[:, 1:])
    )
    return face_flux[:, 1:] - face_flux[:, :-1]


def advance(thickness, potential, zonal, merid_pad, thick_pad, temp_pad):
    heat = thickness * potential
    heat_pad = thick_pad * temp_pad
    new_thick = thickness - COURANT * (
        flux_zonal(thickness, zonal) + flux_merid(thick_pad, merid_pad)
    )
    new_heat = heat - COURANT * (flux_zonal(heat, zonal) + flux_merid(heat_pad, merid_pad))
    return (new_thick, new_heat / new_thick)


def pressure_push(zonal, mid_pressure):
    return zonal - PRESSURE_COEF * (
        jnp.roll(mid_pressure, -1, axis=-1) - jnp.roll(mid_pressure, 1, axis=-1)
    )


def ppm_edges(fields):
    halves = 0.5 * (fields[:, :-1] + fields[:, 1:])
    fourth = 7.0 / 12.0 * (fields[:, 1:-2] + fields[:, 2:-1]) - 1.0 / 12.0 * (
        fields[:, :-3] + fields[:, 3:]
    )
    return jnp.concatenate(
        [fields[:, :1], halves[:, :1], fourth, halves[:, -1:], fields[:, -1:]], axis=1
    )


def remap_columns(fields, thickness, weights):
    levels = thickness.shape[0]
    field_count = fields.shape[0]
    flat_thick = thickness.reshape(levels, -1)
    flat_fields = fields.reshape(field_count, levels, -1)
    top_edges = jnp.cumsum(flat_thick, axis=0) - flat_thick
    surface = jnp.sum(flat_thick, axis=0)
    sigma_edges = (jnp.cumsum(weights) / jnp.sum(weights))[:, None]
    targets = surface[None] * sigma_edges
    previous = jnp.concatenate([jnp.zeros_like(targets[:1]), targets[:-1]], axis=0)
    edge_values = ppm_edges(flat_fields)
    left_edge = edge_values[:, :-1]
    curvature = 6.0 * (flat_fields - 0.5 * (left_edge + edge_values[:, 1:]))
    linear = edge_values[:, 1:] - left_edge + curvature

    def mass_block(edge_block):
        fraction = jnp.clip((edge_block[:, None] - top_edges[None]) / flat_thick[None], 0.0, 1.0)
        collected = []
        for member in range(field_count):
            partial_value = fraction * (
                left_edge[member][None]
                + fraction * (0.5 * linear[member][None] - fraction * curvature[member][None] / 3.0)
            )
            collected.append(jnp.sum(flat_thick[None] * partial_value, axis=1))
        return tuple(collected)

    grouped = targets.reshape(levels // 8, 8, -1)
    masses = lax.map(mass_block, grouped)
    results = []
    for mass in masses:
        mass_below = mass.reshape(levels, -1)
        mass_above = jnp.concatenate([jnp.zeros_like(mass_below[:1]), mass_below[:-1]], axis=0)
        results.append((mass_below - mass_above) / (targets - previous))
    return jnp.stack(results).reshape(fields.shape)


def modes_table(first_wave, wave_count, lon_count):
    wavenumber = first_wave + lax.iota(jnp.int32, wave_count)
    position = lax.iota(jnp.int32, lon_count)
    phase_index = wavenumber[:, None] * position[None, :] % lon_count
    angles = phase_index.astype(jnp.float32) * (2.0 * math.pi / lon_count)
    return (jnp.concatenate([jnp.cos(angles), jnp.sin(angles)], axis=0), wavenumber)


def weighted_spectrum(vectors, limits, modes, wavenumber):
    lon_count = vectors.shape[-1]
    spectrum = jnp.einsum("vi,ki->vk", vectors, modes, precision=HIGHEST)
    factor = jnp.where(wavenumber == 0, 1.0, 2.0) / lon_count
    kept_weight = jnp.where(wavenumber[None, :] <= limits[:, None], factor[None, :], 0.0)
    kept_weight = jnp.concatenate([kept_weight, kept_weight], axis=1)
    return spectrum * kept_weight


def filter_part(vectors, limits, first_wave, wave_count):
    modes, wavenumber = modes_table(first_wave, wave_count, vectors.shape[-1])
    weighted = weighted_spectrum(vectors, limits, modes, wavenumber)
    return jnp.dot(weighted, modes, precision=HIGHEST, preferred_element_type=jnp.float32)


def add_terms(earlier, later):
    return earlier + later


def local(zonal_wind, merid_wind, thickness, potential_temp, cutoff, sigma_weights):
    levels_dev, rows_dev, lon_count = zonal_wind.shape
    band_count = lax.axis_size("lat")
    band_index = lax.axis_index("lat")
    polar_rows = POLAR_BANDS * rows_dev
    all_rows = band_count * rows_dev
    wind_pair = jnp.stack([zonal_wind, merid_wind])
    southern = band_index < POLAR_BANDS
    is_polar = jnp.logical_or(southern, band_index >= band_count - POLAR_BANDS)
    offset = jnp.where(
        southern, band_index * rows_dev, band_index * rows_dev - all_rows + 2 * polar_rows
    )
    offset = jnp.clip(offset, 0, 2 * polar_rows - rows_dev)
    own_limits = lax.dynamic_slice_in_dim(cutoff, offset, rows_dev)
    limits = jnp.broadcast_to(own_limits, (2, levels_dev, rows_dev)).reshape(-1)

    def smoothed(wind_block):
        flat_rows = wind_block.reshape(-1, lon_count)
        return filter_part(flat_rows, limits, 0, KMAX).reshape(wind_block.shape)

    def unchanged(wind_block):
        return wind_block

    wind_pair = lax.cond(is_polar, smoothed, unchanged, wind_pair)
    zonal = wind_pair[0]
    stacked = jnp.stack([thickness, wind_pair[1], potential_temp])
    padded = with_halo(stacked, (("lat", 2),), 1)
    new_thick, new_temp = advance(thickness, potential_temp, zonal, padded[1], padded[0], padded[2])
    own_mass = jnp.sum(new_thick, axis=0)
    upper_mass = prefix(own_mass, "lev", add_terms, jnp.zeros_like(own_mass))
    mid_pressure = upper_mass[None] + jnp.cumsum(new_thick, axis=0) - 0.5 * new_thick
    new_zonal = pressure_push(zonal, mid_pressure)
    outgoing = jnp.stack([new_zonal, new_temp, new_thick])
    columns = lax.all_to_all(outgoing, "lev", split_axis=3, concat_axis=1, tiled=True)
    result = remap_columns(columns[:2], columns[2], sigma_weights)
    return (result[0], result[1])


def solution(mesh):
    in_specs = (
        P("lev", "lat", None),
        P("lev", "lat", None),
        P("lev", "lat", None),
        P("lev", "lat", None),
        P(),
        P(),
    )
    out_specs = (P(None, "lat", "lev"), P(None, "lat", "lev"))
    return jax.shard_map(local, mesh=mesh, in_specs=in_specs, out_specs=out_specs, check_vma=False)
```

profile of v0, /device:TPU:32, one launch (start us, length us, event | category | flops | bytes accessed | tf_op | source)
XLA Modules:
  0.0 282.6 jit_solution(11586409146098346025)
XLA Ops:
  7.2 2.0 pad_maximum_fusion.11
  9.3 1.2 slice_bitcast_fusion.9
  10.5 1.3 pad_maximum_fusion.14
  11.8 1.9 collective-permute-start
  13.8 27.1 %collective-permute-start.1 = (f32[3,4,1,2880]{3,1,2,0:T(4,128)S(1)}, f32[3,4,1,2880]{3,1,2,0:T(4,128)S(1)}, u32[]{:S(2)}, u32[]{:S(2)}) collective-permute-start(f32[3,4,1,2880]{3,1,2,0:T(4,128)S(1)} %copy.84), channel_id=1, source_target_pairs={{16,0},{32,16},{48,32},{64,48},{80,64},{96,80},{112,96},{128,112},... | collective-permute-start | bytes 414728 | tf_op jit(solution)/shard_map/ppermute | solution.py:22
  41.2 1.4 fusion.36
  44.4 0.8 fusion.37
  45.4 62.9 %all-gather.3.cloned.1.call-done = f32[128,2880]{1,0:T(8,128)} async-done(((f32[8,2880]{1,0:T(8,128)}), f32[128,2880]{1,0:T(8,128)}) %all-gather.3.cloned.1.call-update) | async-done | bytes 1474576 | tf_op jit(solution)/shard_map/all_gather | solution.py:29
  108.4 2.4 fusion.15
  111.0 1.2 fusion.35
  112.3 12.1 %copy.79 = f32[3,4,8,2880]{2,1,0,3:T(4,128)} copy(f32[3,4,8,2880]{3,2,1,0:T(8,128)S(1)} %pad_maximum_fusion.8) | data formatting | bytes 2211840 | tf_op jit(solution)/shard_map/stack | solution.py:174
  124.4 22.8 %reshape.137 = f32[16,1,17280]{2,1,0:T(1,128)} reshape(f32[2880,3,4,8]{3,2,1,0:T(4,128)} %bitcast.101) | data formatting | bytes 2211840
  147.2 18.2 %all-to-all-start = ((f32[16,1,17280]{2,1,0:T(1,128)}), f32[16,1,17280]{2,1,0:T(1,128)S(1)}, u32[]{:S(2)}, u32[]{:S(2)}) async-start(f32[16,1,17280]{2,1,0:T(1,128)} %reshape.137), calls=%async_computation | async-start | bytes 2211840 | tf_op jit(solution)/shard_map/all_to_all | solution.py:175
  166.2 0.8 divide_reduce_fusion
  167.0 14.3 %all-to-all-done = f32[16,1,17280]{2,1,0:T(1,128)S(1)} async-done(((f32[16,1,17280]{2,1,0:T(1,128)}), f32[16,1,17280]{2,1,0:T(1,128)S(1)}, u32[]{:S(2)}, u32[]{:S(2)}) %all-to-all-start) | async-done | bytes 1105952 | tf_op jit(solution)/shard_map/all_to_all | solution.py:175
  181.9 3.3 %reduce.4 = f32[16,17280]{1,0:T(8,128)S(1)} reduce(f32[16,1,17280]{2,1,0:T(1,128)S(1)} %all-to-all-done, f32[]{:T(128)} %broadcast.115), dimensions={1}, to_apply=%all_to_all.11.reduce_sub_computation | reduce | bytes 2211844 | tf_op jit(solution)/shard_map/all_to_all | solution.py:175
  185.2 27.2 %reshape.138 = f32[2880,3,4,8]{3,2,1,0:T(4,128)} reshape(f32[16,17280]{1,0:T(8,128)S(1)} %reduce.4) | data formatting | bytes 2211840
  212.4 12.9 %copy.80 = f32[3,4,8,16,180]{4,2,1,3,0:T(8,128)S(1)} copy(f32[3,4,8,16,180]{2,1,0,4,3:T(4,128)} %bitcast.100) | data formatting | bytes 2211840 | tf_op jit(solution)/shard_map/all_to_all | solution.py:175
  225.3 1.1 slice.252
  226.3 1.6 reshape.131
  228.4 0.9 slice_reduce_fusion
  229.7 1.3 reshape_squeeze.3
  231.0 1.1 reduce_window_sum.30
  232.1 1.0 sub.102
  233.2 0.9 broadcast_multiply_fusion
  234.1 0.8 broadcast_multiply_fusion.1
  234.9 1.3 mul.381
  236.2 35.5 %while.24 = (s32[]{:T(128)}, f32[8,8,1440]{2,1,0:T(8,128)}, f32[8,8,1440]{2,1,0:T(8,128)}, f32[1,64,8,180]{3,2,1,0:T(8,128)}, f32[8,8,1440]{2,1,0:T(8,128)}, /*i...) while((s32[]{:T(128)}, f32[8,8,1440]{2,1,0:T(8,128)}, ...), condition=%wide.wide.region_13.14_spmd, body=%wide.wide.region_10.13_spmd.sunk | while | flops 14169602 | bytes 7794801 | solution.py:106
  236.3 0.8 dynamic-slice_bitcast_fusion.3
  237.2 2.2 multiply_reduce_fusion.4
  239.4 0.6 bitcast_dynamic-update-slice_fusion.7
  240.8 0.8 dynamic-slice_bitcast_fusion.3
  241.6 2.2 multiply_reduce_fusion.4
  245.2 0.8 dynamic-slice_bitcast_fusion.3
  246.1 2.2 multiply_reduce_fusion.4
  249.6 0.8 dynamic-slice_bitcast_fusion.3
  250.5 2.2 multiply_reduce_fusion.4
  254.1 0.8 dynamic-slice_bitcast_fusion.3
  255.0 2.2 multiply_reduce_fusion.4
  258.5 0.8 dynamic-slice_bitcast_fusion.3
  259.4 2.2 multiply_reduce_fusion.4
  263.0 0.8 dynamic-slice_bitcast_fusion.3
  263.8 2.2 multiply_reduce_fusion.4
  267.4 0.8 dynamic-slice_bitcast_fusion.3
  268.3 2.2 multiply_reduce_fusion.4
  271.7 1.7 subtract_divide_fusion
  273.4 1.2 squeeze.28
  274.6 1.2 squeeze.29
  (77 shorter events, 15.9 us)
Async XLA Ops:
  7.2 101.2 %all-gather.3.cloned.1.call-start = ((), (), s32[]{:S(2)}) async-start(), calls=%async_computation.1 | async-start | bytes 1601536 | tf_op jit(solution)/shard_map/all_gather | solution.py:29
  9.3 1.2 copy-start.1
  9.3 31.6 %copy-start.2 = (f32[4,8,2880]{2,1,0:T(8,128)S(1)}, f32[4,8,2880]{2,1,0:T(8,128)}, u32[]{:S(2)}) copy-start(f32[4,8,2880]{2,1,0:T(8,128)} %param.15) | copy-start | bytes 1105924
  11.8 30.8 %collective-permute-start = (f32[3,4,1,2880]{3,1,2,0:T(4,128)S(1)}, f32[3,4,1,2880]{3,1,2,0:T(4,128)S(1)}, u32[]{:S(2)}, u32[]{:S(2)}) collective-permute-start(f32[3,4,1,2880]{3,1,2,0:T(4,128)S(1)} %copy.83), channel_id=1, source_target_pairs={{0,16},{16,32},{32,48},{48,64},{64,80},{80,96},{96,112},{112,128},... | collective-permute-start | bytes 414728 | tf_op jit(solution)/shard_map/ppermute | solution.py:21
  13.8 29.5 %collective-permute-start.1 = (f32[3,4,1,2880]{3,1,2,0:T(4,128)S(1)}, f32[3,4,1,2880]{3,1,2,0:T(4,128)S(1)}, u32[]{:S(2)}, u32[]{:S(2)}) collective-permute-start(f32[3,4,1,2880]{3,1,2,0:T(4,128)S(1)} %copy.84), channel_id=1, source_target_pairs={{16,0},{32,16},{48,32},{64,48},{80,64},{96,80},{112,96},{128,112},... | collective-permute-start | bytes 414728 | tf_op jit(solution)/shard_map/ppermute | solution.py:22
  124.4 41.0 %copy-start.3 = (f32[64]{0:T(128)S(1)}, f32[64]{0:T(128)}, u32[]{:S(2)}) copy-start(f32[64]{0:T(128)} %param.17) | copy-start | bytes 772
  147.2 34.2 %all-to-all-start = ((f32[16,1,17280]{2,1,0:T(1,128)}), f32[16,1,17280]{2,1,0:T(1,128)S(1)}, u32[]{:S(2)}, u32[]{:S(2)}) async-start(f32[16,1,17280]{2,1,0:T(1,128)} %reshape.137), calls=%async_computation | async-start | bytes 2211840 | tf_op jit(solution)/shard_map/all_to_all | solution.py:175
Sparse Core Ops, SparseCore 0:
  45.3 63.0 all-gather.2
where the time goes:
time: 284 us; the launch traced here: 283 us
  local copies, waits for them, and re-layouts  103 us (36%)
  waiting for transfers between devices  77.7 us (27%)
  starting transfers between devices  47.2 us (17%)
  other arithmetic  40.5 us (14%)
  between operations  14.3 us (5%)
    all_gather x1, waiting for transfers between devices, prefix(): gathered = lax.all_gather(part, axis)  62.9 us
    unnamed x10, local copies, waits for them, and re-layouts  50.1 us
    ppermute x1, starting transfers between devices, with_halo(): after = lax.ppermute(first, axis, down)  27.1 us
    all_to_all x1, starting transfers between devices, local(): lax.all_to_all(outgoing, 'lev', split_axis=3, concat_axis=1, tiled=True)  18.2 us
    reduce_sum x8, other arithmetic, mass_block(): collected.append(jnp.sum(flat_thick[None] * partial_value, axis=1))  17.5 us
    all_to_all x1, waiting for transfers between devices, local(): lax.all_to_all(outgoing, 'lev', split_axis=3, concat_axis=1, tiled=True)  14.3 us
    all_to_all x2, local copies, waits for them, and re-layouts, local(): lax.all_to_all(outgoing, 'lev', split_axis=3, concat_axis=1, tiled=True)  13.4 us
    another operation x1, local copies, waits for them, and re-layouts, local(): outgoing = jnp.stack([new_zonal, new_temp, new_thick])  12.1 us
  transfers between devices with their start and end apart: 4, of which 3 were waited for; matrix products, arithmetic and copies ran while one was open for 1% of the time, Pallas kernels for 0%

commit v1 on v0

--- a/solution.py
+++ b/solution.py
@@ -172,7 +172,10 @@
     mid_pressure = upper_mass[None] + jnp.cumsum(new_thick, axis=0) - 0.5 * new_thick
     new_zonal = pressure_push(zonal, mid_pressure)
     outgoing = jnp.stack([new_zonal, new_temp, new_thick])
-    columns = lax.all_to_all(outgoing, "lev", split_axis=3, concat_axis=1, tiled=True)
+    columns = jnp.concatenate(
+        lax.all_to_all(jnp.stack(jnp.split(outgoing, lax.axis_size("lev"), axis=3)), "lev", 0, 0),
+        axis=1,
+    )
     result = remap_columns(columns[:2], columns[2], sigma_weights)
     return (result[0], result[1])
 

time: 284 us -> 218 us (0.77)
  local copies, waits for them, and re-layouts: 103 us -> 34.2 us
  waiting for transfers between devices: 77.7 us -> 83.1 us
  other arithmetic: 40.5 us -> 37.3 us
    unnamed x10 -> x25, local copies, waits for them, and re-layouts: 50.1 us -> 10.9 us
    all_to_all x2 -> x0, local copies, waits for them, and re-layouts: 13.4 us -> none  [local(): lax.all_to_all(outgoing, 'lev', split_axis=3, concat_axis=1, tiled=True)]
    another operation x1, local copies, waits for them, and re-layouts: 12.1 us -> 0.73 us  [local(): jnp.stack(jnp.split(outgoing, lax.axis_size('lev'), axis=3))]
    all_to_all x1, waiting for transfers between devices: 14.3 us -> 19.4 us  [local(): lax.all_to_all(jnp.stack(jnp.split(outgoing, lax.axis_size('lev'), axis=3...]
    dynamic_update_slice x16, local copies, waits for them, and re-layouts: 9.97 us -> 5.08 us  [remap_columns(): masses = lax.map(mass_block, grouped)]
    all_to_all x1 -> x0, other arithmetic: 3.27 us -> none  [local(): lax.all_to_all(outgoing, 'lev', split_axis=3, concat_axis=1, tiled=True)]
  transfers between devices with their start and end apart: 4 -> 4, of which waited for: 3 -> 3; matrix products, arithmetic and copies ran while one was open for 1% -> 2% of each run, Pallas kernels for 0% -> 0%
where the time goes in v1:
time: 218 us; the launch traced here: 216 us
  waiting for transfers between devices  83.1 us (38%)
  starting transfers between devices  47.2 us (22%)
  other arithmetic  37.3 us (17%)
  local copies, waits for them, and re-layouts  34.2 us (16%)
  between operations  14.3 us (7%)
    all_gather x1, waiting for transfers between devices, prefix(): gathered = lax.all_gather(part, axis)  62.9 us
    ppermute x1, starting transfers between devices, with_halo(): after = lax.ppermute(first, axis, down)  26.9 us
    all_to_all x1, waiting for transfers between devices, local(): lax.all_to_all(jnp.stack(jnp.split(outgoing, lax.axis_size('lev'), axis=3...  19.4 us
    all_to_all x1, starting transfers between devices, local(): lax.all_to_all(jnp.stack(jnp.split(outgoing, lax.axis_size('lev'), axis=3...  18.3 us
    reduce_sum x8, other arithmetic, mass_block(): collected.append(jnp.sum(flat_thick[None] * partial_value, axis=1))  17.5 us
    unnamed x25, local copies, waits for them, and re-layouts  10.9 us
    sub x8, local copies, waits for them, and re-layouts, mass_block(): edge_block[:, None] - top_edges[None]  6.47 us
    dynamic_update_slice x16, local copies, waits for them, and re-layouts, remap_columns(): masses = lax.map(mass_block, grouped)  5.08 us
  transfers between devices with their start and end apart: 4, of which 3 were waited for; matrix products, arithmetic and copies ran while one was open for 2% of the time, Pallas kernels for 0%

profile of v1, /device:TPU:32, one launch (start us, length us, event | category | flops | bytes accessed | tf_op | source)
XLA Modules:
  0.0 216.3 jit_solution(9129141795702191568)
XLA Ops:
  7.2 2.0 pad_maximum_fusion.11
  9.3 1.2 slice_bitcast_fusion.9
  10.8 1.9 collective-permute-start
  12.7 26.9 %collective-permute-start.1 = (f32[3,4,1,2880]{3,2,1,0:T(1,128)S(1)}, f32[3,4,1,2880]{3,2,1,0:T(1,128)S(1)}, u32[]{:S(2)}, u32[]{:S(2)}) collective-permute-start(f32[3,4,1,2880]{3,2,1,0:T(1,128)S(1)} %get-tuple-element.179), channel_id=1, source_target_pairs={{16,0},{32,16},{48,32},{64,48},{80,64},{96,80},{112,96},{128,112},... | collective-permute-start | bytes 414728 | tf_op jit(solution)/shard_map/ppermute | solution.py:22
  39.9 1.4 fusion.36
  41.4 0.8 collective-permute-done.1
  43.1 0.8 fusion.53
  44.2 62.9 %all-gather.3.cloned.1.call-done = f32[128,2880]{1,0:T(8,128)} async-done(((f32[8,2880]{1,0:T(8,128)}), f32[128,2880]{1,0:T(8,128)}) %all-gather.3.cloned.1.call-update) | async-done | bytes 1474576 | tf_op jit(solution)/shard_map/all_gather | solution.py:29
  107.1 2.4 %fusion.15 = f32[4,8,2880]{2,1,0:T(8,128)S(1)} fusion(f32[4,8,2880]{2,1,0:T(8,128)S(1)} %get-tuple-element.159, f32[8,2880]{1,0:T(8,128)S(1)} %get-tuple-element.125), kind=kOutput, calls=%fused_computation.34 | output fusion | flops 552960 | bytes 829440 | tf_op jit(solution)/shard_map/jit(cumsum)/reduce_window_sum | solution.py:172
  109.8 1.2 fusion.35
  112.4 0.7 fusion.50
  113.1 0.7 fusion.49
  113.9 0.7 fusion.48
  116.8 0.7 fusion.44
  119.0 0.7 fusion.41
  120.4 0.7 fusion.39
  122.6 18.3 %all-to-all-start = ((f32[16,3,4,8,180]{4,3,2,1,0:T(8,128)}), f32[16,3,4,8,180]{4,3,2,1,0:T(8,128)S(1)}, u32[]{:S(2)}, u32[]{:S(2)}) async-start(f32[16,3,4,8,180]{4,3,2,1,0:T(8,128)} %fusion.37), calls=%async_computation | async-start | bytes 3145728 | tf_op jit(solution)/shard_map/all_to_all | solution.py:176
  141.7 0.8 divide_reduce_fusion
  143.2 19.4 %all-to-all-done = f32[16,3,4,8,180]{4,3,2,1,0:T(8,128)S(1)} async-done(((f32[16,3,4,8,180]{4,3,2,1,0:T(8,128)}), f32[16,3,4,8,180]{4,3,2,1,0:T(8,128)S(1)}, u32[]{:S(2)}, u32[]{:S(2)}) %all-to-all-start) | async-done | bytes 1105952 | tf_op jit(solution)/shard_map/all_to_all | solution.py:176
  162.7 1.1 copy.20
  163.7 1.6 reshape.136
  165.8 0.9 slice_reduce_fusion
  167.2 1.3 reshape_squeeze.3
  168.4 1.1 reduce_window_sum.30
  169.5 1.0 sub.102
  170.6 1.5 broadcast_multiply_fusion
  172.1 1.5 broadcast_multiply_fusion.1
  173.7 1.3 mul.381
  174.9 30.7 %while.24 = (s32[]{:T(128)}, f32[8,8,1440]{2,1,0:T(8,128)S(1)}, f32[8,8,1440]{2,1,0:T(8,128)}, f32[1,64,8,180]{3,2,1,0:T(8,128)}, f32[8,8,1440]{2,1,0:T(8,128)},...) while((s32[]{:T(128)}, f32[8,8,1440]{2,1,0:T(8,128)S(1)}, ...), condition=%wide.wide.region_13.14_spmd, body=%wide.wide.region_10.13_spmd.sunk | while | flops 14169602 | bytes 7797365 | solution.py:106
  175.1 0.8 dynamic-slice_bitcast_fusion.3
  175.9 2.2 %multiply_reduce_fusion.4 = (f32[8,1440]{1,0:T(8,128)S(1)}, f32[8,1440]{1,0:T(8,128)S(1)}) fusion(f32[64,1440]{1,0:T(8,128)S(1)} %get-tuple-element.335, f32[64,1440]{1,0:T(8,128)S(1)} %get-tuple-element.336, f32[64,1440]{1,0:T(8,128)S(1)} %get-tuple-element.337, f32[64,1440]{1,0:T(8,128)S(1)} %get-tuple-element.391, ...), kind=kLoop, calls=%fused_computation.21.clone.clone.1 | loop fusion | flops 13985280 | bytes 3087360 | tf_op jit(solution)/shard_map/while/body/eval_jaxpr/reduce_sum | solution.py:102
  178.9 0.8 dynamic-slice_bitcast_fusion.3
  179.8 2.2 %multiply_reduce_fusion.4 = (f32[8,1440]{1,0:T(8,128)S(1)}, f32[8,1440]{1,0:T(8,128)S(1)}) fusion(f32[64,1440]{1,0:T(8,128)S(1)} %get-tuple-element.335, f32[64,1440]{1,0:T(8,128)S(1)} %get-tuple-element.336, f32[64,1440]{1,0:T(8,128)S(1)} %get-tuple-element.337, f32[64,1440]{1,0:T(8,128)S(1)} %get-tuple-element.391, ...), kind=kLoop, calls=%fused_computation.21.clone.clone.1 | loop fusion | flops 13985280 | bytes 3087360 | tf_op jit(solution)/shard_map/while/body/eval_jaxpr/reduce_sum | solution.py:102
  182.7 0.8 dynamic-slice_bitcast_fusion.3
  183.6 2.2 %multiply_reduce_fusion.4 = (f32[8,1440]{1,0:T(8,128)S(1)}, f32[8,1440]{1,0:T(8,128)S(1)}) fusion(f32[64,1440]{1,0:T(8,128)S(1)} %get-tuple-element.335, f32[64,1440]{1,0:T(8,128)S(1)} %get-tuple-element.336, f32[64,1440]{1,0:T(8,128)S(1)} %get-tuple-element.337, f32[64,1440]{1,0:T(8,128)S(1)} %get-tuple-element.391, ...), kind=kLoop, calls=%fused_computation.21.clone.clone.1 | loop fusion | flops 13985280 | bytes 3087360 | tf_op jit(solution)/shard_map/while/body/eval_jaxpr/reduce_sum | solution.py:102
  186.6 0.8 dynamic-slice_bitcast_fusion.3
  187.4 2.2 %multiply_reduce_fusion.4 = (f32[8,1440]{1,0:T(8,128)S(1)}, f32[8,1440]{1,0:T(8,128)S(1)}) fusion(f32[64,1440]{1,0:T(8,128)S(1)} %get-tuple-element.335, f32[64,1440]{1,0:T(8,128)S(1)} %get-tuple-element.336, f32[64,1440]{1,0:T(8,128)S(1)} %get-tuple-element.337, f32[64,1440]{1,0:T(8,128)S(1)} %get-tuple-element.391, ...), kind=kLoop, calls=%fused_computation.21.clone.clone.1 | loop fusion | flops 13985280 | bytes 3087360 | tf_op jit(solution)/shard_map/while/body/eval_jaxpr/reduce_sum | solution.py:102
  190.4 0.8 dynamic-slice_bitcast_fusion.3
  191.3 2.2 %multiply_reduce_fusion.4 = (f32[8,1440]{1,0:T(8,128)S(1)}, f32[8,1440]{1,0:T(8,128)S(1)}) fusion(f32[64,1440]{1,0:T(8,128)S(1)} %get-tuple-element.335, f32[64,1440]{1,0:T(8,128)S(1)} %get-tuple-element.336, f32[64,1440]{1,0:T(8,128)S(1)} %get-tuple-element.337, f32[64,1440]{1,0:T(8,128)S(1)} %get-tuple-element.391, ...), kind=kLoop, calls=%fused_computation.21.clone.clone.1 | loop fusion | flops 13985280 | bytes 3087360 | tf_op jit(solution)/shard_map/while/body/eval_jaxpr/reduce_sum | solution.py:102
  194.3 0.8 dynamic-slice_bitcast_fusion.3
  195.1 2.2 %multiply_reduce_fusion.4 = (f32[8,1440]{1,0:T(8,128)S(1)}, f32[8,1440]{1,0:T(8,128)S(1)}) fusion(f32[64,1440]{1,0:T(8,128)S(1)} %get-tuple-element.335, f32[64,1440]{1,0:T(8,128)S(1)} %get-tuple-element.336, f32[64,1440]{1,0:T(8,128)S(1)} %get-tuple-element.337, f32[64,1440]{1,0:T(8,128)S(1)} %get-tuple-element.391, ...), kind=kLoop, calls=%fused_computation.21.clone.clone.1 | loop fusion | flops 13985280 | bytes 3087360 | tf_op jit(solution)/shard_map/while/body/eval_jaxpr/reduce_sum | solution.py:102
  198.1 0.8 dynamic-slice_bitcast_fusion.3
  199.0 2.2 %multiply_reduce_fusion.4 = (f32[8,1440]{1,0:T(8,128)S(1)}, f32[8,1440]{1,0:T(8,128)S(1)}) fusion(f32[64,1440]{1,0:T(8,128)S(1)} %get-tuple-element.335, f32[64,1440]{1,0:T(8,128)S(1)} %get-tuple-element.336, f32[64,1440]{1,0:T(8,128)S(1)} %get-tuple-element.337, f32[64,1440]{1,0:T(8,128)S(1)} %get-tuple-element.391, ...), kind=kLoop, calls=%fused_computation.21.clone.clone.1 | loop fusion | flops 13985280 | bytes 3087360 | tf_op jit(solution)/shard_map/while/body/eval_jaxpr/reduce_sum | solution.py:102
  201.9 0.8 dynamic-slice_bitcast_fusion.3
  202.8 2.2 %multiply_reduce_fusion.4 = (f32[8,1440]{1,0:T(8,128)S(1)}, f32[8,1440]{1,0:T(8,128)S(1)}) fusion(f32[64,1440]{1,0:T(8,128)S(1)} %get-tuple-element.335, f32[64,1440]{1,0:T(8,128)S(1)} %get-tuple-element.336, f32[64,1440]{1,0:T(8,128)S(1)} %get-tuple-element.337, f32[64,1440]{1,0:T(8,128)S(1)} %get-tuple-element.391, ...), kind=kLoop, calls=%fused_computation.21.clone.clone.1 | loop fusion | flops 13985280 | bytes 3087360 | tf_op jit(solution)/shard_map/while/body/eval_jaxpr/reduce_sum | solution.py:102
  205.6 1.5 subtract_divide_fusion
  207.1 1.2 squeeze.28
  208.3 1.2 squeeze.29
  (88 shorter events, 18.4 us)
Async XLA Ops:
  7.2 99.9 %all-gather.3.cloned.1.call-start = ((), (), s32[]{:S(2)}) async-start(), calls=%async_computation.1 | async-start | bytes 1601536 | tf_op jit(solution)/shard_map/all_gather | solution.py:29
  9.3 1.2 copy-start.1
  9.3 1.3 copy-start.2
  10.8 30.6 %collective-permute-start = (f32[3,4,1,2880]{3,2,1,0:T(1,128)S(1)}, f32[3,4,1,2880]{3,2,1,0:T(1,128)S(1)}, u32[]{:S(2)}, u32[]{:S(2)}) collective-permute-start(f32[3,4,1,2880]{3,2,1,0:T(1,128)S(1)} %get-tuple-element.178), channel_id=1, source_target_pairs={{0,16},{16,32},{32,48},{48,64},{64,80},{80,96},{96,112},{112,128},... | collective-permute-start | bytes 414728 | tf_op jit(solution)/shard_map/ppermute | solution.py:21
  12.7 29.5 %collective-permute-start.1 = (f32[3,4,1,2880]{3,2,1,0:T(1,128)S(1)}, f32[3,4,1,2880]{3,2,1,0:T(1,128)S(1)}, u32[]{:S(2)}, u32[]{:S(2)}) collective-permute-start(f32[3,4,1,2880]{3,2,1,0:T(1,128)S(1)} %get-tuple-element.179), channel_id=1, source_target_pairs={{16,0},{32,16},{48,32},{64,48},{80,64},{96,80},{112,96},{128,112},... | collective-permute-start | bytes 414728 | tf_op jit(solution)/shard_map/ppermute | solution.py:22
  122.6 18.4 %copy-start.5 = (f32[64]{0:T(128)S(1)}, f32[64]{0:T(128)}, u32[]{:S(2)}) copy-start(f32[64]{0:T(128)} %param.17) | copy-start | bytes 772
  122.6 40.0 %all-to-all-start = ((f32[16,3,4,8,180]{4,3,2,1,0:T(8,128)}), f32[16,3,4,8,180]{4,3,2,1,0:T(8,128)S(1)}, u32[]{:S(2)}, u32[]{:S(2)}) async-start(f32[16,3,4,8,180]{4,3,2,1,0:T(8,128)} %fusion.37), calls=%async_computation | async-start | bytes 3145728 | tf_op jit(solution)/shard_map/all_to_all | solution.py:176
  142.5 21.2 %copy-start.3 = (f32[64]{0:T(128)}, f32[64]{0:T(128)S(1)}, u32[]{:S(2)}) copy-start(f32[64]{0:T(128)S(1)} %divide_reduce_fusion) | copy-start | bytes 772
  174.9 30.7 %copy-start.4 = (f32[64]{0:T(128)S(1)}, f32[64]{0:T(128)}, u32[]{:S(2)}) copy-start(f32[64]{0:T(128)} %copy-done.3) | copy-start | bytes 772
Sparse Core Ops, SparseCore 0:
  44.0 63.0 all-gather.2
